TPU v7x, 128 devices: a whole 4x4x4 slice. The times are simulated.
128 devices in a mesh: seq: 32 (over z_hi, y, x), ch: 4 (over z_lo, core).
Axes of the slice: x: 4, y: 4, z: 4 (z_hi: 2, z_lo: 2; z = z_hi * 2 + z_lo), core: 2. Of those that a mesh axis runs over, the one named last changes fastest.
Arguments:
- tokens: bfloat16 [262144, 512], P('seq', 'ch'), may hold values from -6 to 6
- gate: bfloat16 [262144, 512], P('seq', 'ch'), may hold values from -6 to 6
- cotangent: bfloat16 [262144, 512], P('seq', 'ch'), may hold values from -6 to 6
- w_first: bfloat16 [1024, 1024], replicated, may hold values from -0.1875 to 0.1875
- w_second: bfloat16 [256, 256], replicated, may hold values from -0.375 to 0.375
Outputs:
- mixed: bfloat16 [262144, 512], P('seq', 'ch')
- grad_tokens: bfloat16 [262144, 512], P('seq', 'ch')
- grad_gate: bfloat16 [262144, 512], P('seq', 'ch')
- grad_first: float32 [1024, 1024], replicated
- grad_second: float32 [256, 256], replicated
All inputs are finite; a program needn't handle non-finite values.
Results may differ from a plain program's by a relative error of at most 0.0058.
Values may be sent and summed in bfloat16 or wider, within the bound.
No kernel may reach another device: no remote copies, remote signals or barrier semaphores. Data moves between devices by JAX's collectives and lax.ppermute only.
A program may use at most 128 MiB of HBM per device.

v0:
```python
import jax
import jax.numpy as jnp
from jax import lax
from jax.sharding import PartitionSpec as P


def local(tokens, gate, cotangent, w_first, w_second):
    seq_count = lax.axis_size("seq")
    chan_count = lax.axis_size("ch")
    width = tokens.shape[1]
    block = w_first.shape[0]
    local_blocks = tokens.shape[0] // block
    all_blocks = local_blocks * seq_count
    x_blocks = tokens.reshape(local_blocks, block, width)
    gate_f = gate.reshape(local_blocks, block, width).astype(jnp.float32)
    cot_blocks = cotangent.reshape(local_blocks, block, width)
    first = jnp.einsum("jk,ikc->ijc", w_first, x_blocks, preferred_element_type=jnp.float32)
    sig = jax.nn.sigmoid(gate_f)
    act = gate_f * sig
    slope = sig * (1.0 + gate_f * (1.0 - sig))
    hidden = (first * act).astype(jnp.bfloat16)
    hidden_t = lax.all_to_all(hidden, "seq", split_axis=1, concat_axis=0, tiled=True)
    mixed_t = jnp.einsum(
        "il,ljc->ijc", w_second, hidden_t, preferred_element_type=jnp.float32
    ).astype(jnp.bfloat16)
    mixed = lax.all_to_all(mixed_t, "seq", split_axis=0, concat_axis=1, tiled=True)
    cot_t = lax.all_to_all(cot_blocks, "seq", split_axis=1, concat_axis=0, tiled=True)
    grad_hidden_t = jnp.einsum(
        "il,ijc->ljc", w_second, cot_t, preferred_element_type=jnp.float32
    ).astype(jnp.bfloat16)
    grad_hidden = lax.all_to_all(grad_hidden_t, "seq", split_axis=0, concat_axis=1, tiled=True)
    second_term = jnp.einsum("ijc,ljc->il", cot_t, hidden_t, preferred_element_type=jnp.float32)
    gh_float = grad_hidden.astype(jnp.float32)
    grad_first_act = (gh_float * act).astype(jnp.bfloat16)
    grad_gate = (gh_float * first * slope).astype(jnp.bfloat16)
    grad_tokens = jnp.einsum(
        "jk,ijc->ikc", w_first, grad_first_act, preferred_element_type=jnp.float32
    ).astype(jnp.bfloat16)
    first_term = jnp.einsum(
        "ijc,ikc->jk", grad_first_act, x_blocks, preferred_element_type=jnp.float32
    )
    first_sum, second_sum = lax.psum((first_term, second_term), ("seq", "ch"))
    total_width = width * chan_count
    grad_first = first_sum / jnp.sqrt(jnp.float32(all_blocks * total_width))
    grad_second = second_sum / jnp.sqrt(jnp.float32(block * total_width))
    rows = local_blocks * block
    return (
        mixed.reshape(rows, width),
        grad_tokens.reshape(rows, width),
        grad_gate.reshape(rows, width),
        grad_first,
        grad_second,
    )


def solution(mesh):
    return jax.shard_map(
        local,
        mesh=mesh,
        in_specs=(P("seq", "ch"), P("seq", "ch"), P("seq", "ch"), P(), P()),
        out_specs=(P("seq", "ch"), P("seq", "ch"), P("seq", "ch"), P(), P()),
        check_vma=False,
    )
```

profile of v0, /device:TPU:1, one launch (start us, length us, event | category | flops | bytes accessed | tf_op | source)
XLA Modules:
  0.0 332.1 jit_solution(3215558701580187851)
XLA Ops:
  7.2 0.0 copy-start
  7.2 3.1 copy.85
  10.3 0.0 copy-start.6
  10.3 39.3 %all_to_all.60 = bf16[8,1024,128]{2,0,1:T(8,128)(2,1)S(1)} all-to-all(bf16[8,1024,128]{2,0,1:T(8,128)(2,1)S(1)} %copy.85), channel_id=1, replica_groups=mesh['seq'=32,'ch'=4] {'seq'}, dimensions={1} | all-to-all | bytes 4194304 | tf_op jit(solution)/shard_map/all_to_all | solution.py:27
  49.6 0.0 copy-start.2
  49.6 1.4 copy-done.2
  51.0 0.0 copy-done.6
  51.0 0.7 fusion.14
  51.7 2.7 copy.89
  54.4 4.8 %all-to-all-start.3 = ((bf16[256,32,128]{2,1,0:T(8,128)(2,1)}), bf16[256,32,128]{2,1,0:T(8,128)(2,1)}, u32[]{:S(2)}, u32[]{:S(2)}) async-start(bf16[256,32,128]{2,1,0:T(8,128)(2,1)} %copy.89), calls=%async_computation.3 | async-start | bytes 4194304 | tf_op jit(solution)/shard_map/all_to_all | solution.py:31
  59.2 4.1 %copy.78 = f32[8,1024,128]{1,2,0:T(8,128)} copy(bf16[8,1024,128]{2,1,0:T(8,128)(2,1)} %bitcast.77) | data formatting | bytes 6291456 | tf_op jit(solution)/shard_map/convert_element_type | solution.py:15
  63.3 23.5 %all-to-all-done.3 = bf16[256,32,128]{2,1,0:T(8,128)(2,1)} async-done(((bf16[256,32,128]{2,1,0:T(8,128)(2,1)}), bf16[256,32,128]{2,1,0:T(8,128)(2,1)}, u32[]{:S(2)}, u32[]{:S(2)}) %all-to-all-start.3) | async-done | bytes 2097184 | tf_op jit(solution)/shard_map/all_to_all | solution.py:31
  86.8 2.1 convert_bitcast_fusion
  88.9 2.6 copy.90
  91.6 5.4 %copy.91 = f32[8,1024,128]{1,2,0:T(8,128)} copy(f32[8,1024,128]{2,1,0:T(8,128)} %bitcast.71) | data formatting | bytes 8388608 | tf_op jit(solution)/shard_map/convert_element_type | solution.py:33
  97.0 0.0 copy-done
  97.0 8.7 %fusion.2 = (bf16[8,1024,128]{1,2,0:T(8,128)(2,1)}, bf16[8,1024,128]{1,2,0:T(8,128)(2,1)}, bf16[8,1024,128]{1,2,0:T(8,128)(2,1)}) fusion(f32[8,1024,128]{1,2,0:T(8,128)} %copy.91, f32[8,1024,128]{1,2,0:T(8,128)} %copy.78, bf16[8,1024,128]{2,1,0:T(8,128)(2,1)S(1)} %bitcast.69, bf16[1024,1024]{1,0:T(8,128)(2,1)} %param.8), kind=kOutput, calls=%fused_computation.5 | convolution fusion | flops 2163212288 | bytes 18874368 | tf_op jit(solution)/shard_map/jk,ikc->ijc/dot_general | solution.py:17
  105.6 4.2 %copy.79 = bf16[8,1024,128]{2,0,1:T(8,128)(2,1)} copy(bf16[8,1024,128]{1,2,0:T(8,128)(2,1)} %get-tuple-element.33) | data formatting | bytes 4194304 | tf_op jit(solution)/shard_map/convert_element_type | solution.py:21
  109.8 4.8 %all-to-all-start = ((bf16[8,1024,128]{2,0,1:T(8,128)(2,1)}), bf16[8,1024,128]{2,0,1:T(8,128)(2,1)}, u32[]{:S(2)}, u32[]{:S(2)}) async-start(bf16[8,1024,128]{2,0,1:T(8,128)(2,1)} %copy.79), calls=%async_computation | async-start | bytes 4194304 | tf_op jit(solution)/shard_map/all_to_all | solution.py:22
  114.6 0.2 all-reduce.3.cloned.1.call-start
  114.8 6.0 %convolution_bitcast_fusion = f32[1024,1024]{1,0:T(8,128)} fusion(bf16[8,1024,128]{1,2,0:T(8,128)(2,1)} %get-tuple-element.34, bf16[8,1024,128]{2,1,0:T(8,128)(2,1)S(1)} %bitcast.70), kind=kOutput, calls=%fused_computation.9 | convolution fusion | flops 2147483648 | bytes 8388608 | tf_op jit(solution)/shard_map/ijc,ikc->jk/dot_general | solution.py:39
  120.8 19.4 %all-to-all-done = bf16[8,1024,128]{2,0,1:T(8,128)(2,1)} async-done(((bf16[8,1024,128]{2,0,1:T(8,128)(2,1)}), bf16[8,1024,128]{2,0,1:T(8,128)(2,1)}, u32[]{:S(2)}, u32[]{:S(2)}) %all-to-all-start) | async-done | bytes 2097184 | tf_op jit(solution)/shard_map/all_to_all | solution.py:22
  140.2 0.0 copy-start.3
  140.2 2.2 copy.81
  142.4 0.0 copy-start.4
  142.4 1.3 copy-done.4
  143.7 0.0 copy-done.3
  143.7 1.7 fusion.21
  145.4 0.0 copy-start.5
  145.4 0.0 all-reduce.3.cloned.1.call-update
  145.4 1.6 copy-done.5
  147.0 3.0 convert_bitcast_fusion.2
  150.0 4.6 %copy.83 = bf16[256,32,128]{2,1,0:T(8,128)(2,1)} copy(bf16[256,32,128]{0,2,1:T(8,128)(2,1)} %convert_bitcast_fusion.2) | data formatting | bytes 4194304 | tf_op jit(solution)/shard_map/convert_element_type | solution.py:25
  154.6 5.4 %all-to-all-start.1 = ((bf16[256,32,128]{2,1,0:T(8,128)(2,1)}), bf16[256,32,128]{2,1,0:T(8,128)(2,1)S(1)}, u32[]{:S(2)}, u32[]{:S(2)}) async-start(bf16[256,32,128]{2,1,0:T(8,128)(2,1)} %copy.83), calls=%async_computation.1 | async-start | bytes 4194304 | tf_op jit(solution)/shard_map/all_to_all | solution.py:26
  160.0 3.9 %copy.95 = bf16[8,1024,128]{2,1,0:T(8,128)(2,1)} copy(bf16[8,1024,128]{1,2,0:T(8,128)(2,1)} %get-tuple-element.32) | data formatting | bytes 4194304 | tf_op jit(solution)/shard_map/convert_element_type | solution.py:35
  163.9 6.0 %convert_bitcast_fusion.1 = bf16[8,1024,128]{1,2,0:T(8,128)(2,1)} fusion(bf16[8,1024,128]{1,2,0:T(8,128)(2,1)} %get-tuple-element.34, bf16[1024,1024]{1,0:T(8,128)(2,1)} %param.8), kind=kOutput, calls=%fused_computation.19 | convolution fusion | flops 2148532224 | bytes 6291456 | tf_op jit(solution)/shard_map/jk,ijc->ikc/dot_general | solution.py:36
  169.9 3.9 %copy.92 = bf16[8,1024,128]{2,1,0:T(8,128)(2,1)} copy(bf16[8,1024,128]{1,2,0:T(8,128)(2,1)} %convert_bitcast_fusion.1) | data formatting | bytes 4194304 | tf_op jit(solution)/shard_map/convert_element_type | solution.py:38
  173.8 15.1 %all-to-all-done.1 = bf16[256,32,128]{2,1,0:T(8,128)(2,1)S(1)} async-done(((bf16[256,32,128]{2,1,0:T(8,128)(2,1)}), bf16[256,32,128]{2,1,0:T(8,128)(2,1)S(1)}, u32[]{:S(2)}, u32[]{:S(2)}) %all-to-all-start.1) | async-done | bytes 2097184 | tf_op jit(solution)/shard_map/all_to_all | solution.py:26
  188.9 1.8 copy.84
  190.6 128.4 %all-reduce.3.cloned.1.call-done = (f32[1024,1024]{1,0:T(8,128)}, f32[256,256]{0,1:T(8,128)}) async-done(((f32[1024,1024]{1,0:T(8,128)}, f32[256,256]{0,1:T(8,128)}), (f32[1024,1024]{1,0:T(8,128)}, f32[256,256]{0,1:T(8,128)})) %all-reduce.3.cloned.1.call-update) | async-done | bytes 4456464 | tf_op jit(solution)/shard_map/psum | solution.py:42
  319.1 0.0 copy-start.7
  319.1 0.0 copy-start.1
  319.1 5.3 %broadcast_multiply_fusion = f32[1024,1024]{1,0:T(8,128)} fusion(f32[1024,1024]{1,0:T(8,128)} %get-tuple-element.30), kind=kLoop, calls=%fused_computation.18 | loop fusion | flops 1048576 | bytes 8388608 | tf_op jit(solution)/shard_map/div | solution.py:44
  324.3 0.0 copy-done.7
  324.4 0.8 copy.98
  325.2 0.0 copy-done.1
  (1 shorter events, 0.0 us)
Async XLA Ops:
  7.2 89.8 %copy-start = (bf16[8192,128]{1,0:T(8,128)(2,1)S(1)}, bf16[8192,128]{1,0:T(8,128)(2,1)}, u32[]{:S(2)}) copy-start(bf16[8192,128]{1,0:T(8,128)(2,1)} %param.5) | copy-start | bytes 6291460
  10.3 40.7 %copy-start.6 = (bf16[256,256]{1,0:T(8,128)(2,1)S(1)}, bf16[256,256]{1,0:T(8,128)(2,1)}, u32[]{:S(2)}) copy-start(bf16[256,256]{1,0:T(8,128)(2,1)} %param.9) | copy-start | bytes 393220
  49.6 1.4 copy-start.2
  54.4 32.4 %all-to-all-start.3 = ((bf16[256,32,128]{2,1,0:T(8,128)(2,1)}), bf16[256,32,128]{2,1,0:T(8,128)(2,1)}, u32[]{:S(2)}, u32[]{:S(2)}) async-start(bf16[256,32,128]{2,1,0:T(8,128)(2,1)} %copy.89), calls=%async_computation.3 | async-start | bytes 4194304 | tf_op jit(solution)/shard_map/all_to_all | solution.py:31
  109.8 30.4 %all-to-all-start = ((bf16[8,1024,128]{2,0,1:T(8,128)(2,1)}), bf16[8,1024,128]{2,0,1:T(8,128)(2,1)}, u32[]{:S(2)}, u32[]{:S(2)}) async-start(bf16[8,1024,128]{2,0,1:T(8,128)(2,1)} %copy.79), calls=%async_computation | async-start | bytes 4194304 | tf_op jit(solution)/shard_map/all_to_all | solution.py:22
  114.6 204.5 %all-reduce.3.cloned.1.call-start = ((), (), s32[]{:S(2)}) async-start(), calls=%async_computation.4 | async-start | bytes 8912896 | tf_op jit(solution)/shard_map/psum | solution.py:42
  140.2 3.5 %copy-start.3 = (bf16[8,1024,128]{2,0,1:T(8,128)(2,1)S(1)}, bf16[8,1024,128]{2,0,1:T(8,128)(2,1)}, u32[]{:S(2)}) copy-start(bf16[8,1024,128]{2,0,1:T(8,128)(2,1)} %copy-done.2) | copy-start | bytes 6291460
  142.4 1.3 copy-start.4
  145.4 1.6 copy-start.5
  154.6 34.3 %all-to-all-start.1 = ((bf16[256,32,128]{2,1,0:T(8,128)(2,1)}), bf16[256,32,128]{2,1,0:T(8,128)(2,1)S(1)}, u32[]{:S(2)}, u32[]{:S(2)}) async-start(bf16[256,32,128]{2,1,0:T(8,128)(2,1)} %copy.83), calls=%async_computation.1 | async-start | bytes 4194304 | tf_op jit(solution)/shard_map/all_to_all | solution.py:26
  319.1 5.3 %copy-start.7 = (f32[256,256]{0,1:T(8,128)S(1)}, f32[256,256]{0,1:T(8,128)}, u32[]{:S(2)}) copy-start(f32[256,256]{0,1:T(8,128)} %get-tuple-element.31) | copy-start | bytes 786436
  319.1 6.1 %copy-start.1 = (bf16[8192,128]{1,0:T(8,128)(2,1)S(1)}, bf16[8192,128]{1,0:T(8,128)(2,1)}, u32[]{:S(2)}) copy-start(bf16[8192,128]{1,0:T(8,128)(2,1)} %param.5) | copy-start | bytes 6291460
Sparse Core Ops, SparseCore 0:
  145.5 173.4 all-reduce.2
where the time goes:
time: 333 us; the launch traced here: 332 us
  waiting for transfers between devices  186 us (56%)
  local copies, waits for them, and re-layouts  43.6 us (13%)
  blocking collectives  39.3 us (12%)
  matrix products  26 us (8%)
  starting transfers between devices  15.2 us (5%)
  between operations  14.1 us (4%)
  other arithmetic  7.44 us (2%)
    psum x1, waiting for transfers between devices, local(): first_sum, second_sum = lax.psum((first_term, second_term), ('seq', 'ch'))  128 us
    all_to_all x1, blocking collectives, local(): lax.all_to_all(cot_blocks, 'seq', split_axis=1, concat_axis=0, tiled=True)  39.3 us
    all_to_all x1, waiting for transfers between devices, local(): lax.all_to_all(grad_hidden_t, 'seq', split_axis=0, concat_axis=1, tiled=T...  23.5 us
    all_to_all x1, waiting for transfers between devices, local(): lax.all_to_all(hidden, 'seq', split_axis=1, concat_axis=0, tiled=True)  19.4 us
    all_to_all x1, waiting for transfers between devices, local(): lax.all_to_all(mixed_t, 'seq', split_axis=0, concat_axis=1, tiled=True)  15.1 us
    dot_general x1, matrix products, local(): jnp.einsum('jk,ikc->ijc', w_first, x_blocks, preferred_element_type=jnp.f...  8.67 us
    convert_element_type x2, local copies, waits for them, and re-layouts, local(): gh_float = grad_hidden.astype(jnp.float32)  8.05 us
  transfers between devices with their start and end apart: 4, of which 4 were waited for; matrix products, arithmetic and copies ran while one was open for 10% of the time, Pallas kernels for 0%

commit v1 on v0

--- a/solution.py
+++ b/solution.py
@@ -2,6 +2,11 @@
 import jax.numpy as jnp
 from jax import lax
 from jax.sharding import PartitionSpec as P
+
+
+def axis_by_axis(value, axis_one, axis_two):
+    partial = lax.psum(value, axis_one)
+    return lax.psum(partial, axis_two)
 
 
 def local(tokens, gate, cotangent, w_first, w_second):
@@ -39,7 +44,7 @@
     first_term = jnp.einsum(
         "ijc,ikc->jk", grad_first_act, x_blocks, preferred_element_type=jnp.float32
     )
-    first_sum, second_sum = lax.psum((first_term, second_term), ("seq", "ch"))
+    first_sum, second_sum = axis_by_axis((first_term, second_term), "seq", "ch")
     total_width = width * chan_count
     grad_first = first_sum / jnp.sqrt(jnp.float32(all_blocks * total_width))
     grad_second = second_sum / jnp.sqrt(jnp.float32(block * total_width))

time: 333 us -> 639 us (1.92)
  waiting for transfers between devices: 186 us -> 491 us
    psum x1 -> x2, waiting for transfers between devices: 128 us -> 443 us  [the longest x1 345 us: axis_by_axis(): partial = lax.psum(value, axis_one)]
    all_to_all x1, waiting for transfers between devices: 15.1 us -> 4.45 us  [local(): lax.all_to_all(mixed_t, 'seq', split_axis=0, concat_axis=1, tiled=True)]
  transfers between devices with their start and end apart: 4 -> 5, of which waited for: 4 -> 5; matrix products, arithmetic and copies ran while one was open for 10% -> 5% of each run, Pallas kernels for 0% -> 0%
where the time goes in v1:
time: 639 us; the launch traced here: 638 us
  waiting for transfers between devices  491 us (77%)
  local copies, waits for them, and re-layouts  43.6 us (7%)
  blocking collectives  39.3 us (6%)
  matrix products  26 us (4%)
  starting transfers between devices  17.3 us (3%)
  between operations  14.1 us (2%)
  other arithmetic  7.44 us (1%)
    psum x1, waiting for transfers between devices, axis_by_axis(): partial = lax.psum(value, axis_one)  345 us
    psum x1, waiting for transfers between devices, axis_by_axis(): return lax.psum(partial, axis_two)  97.9 us
    all_to_all x1, blocking collectives, local(): lax.all_to_all(cot_blocks, 'seq', split_axis=1, concat_axis=0, tiled=True)  39.3 us
    all_to_all x1, waiting for transfers between devices, local(): lax.all_to_all(grad_hidden_t, 'seq', split_axis=0, concat_axis=1, tiled=T...  23.5 us
    all_to_all x1, waiting for transfers between devices, local(): lax.all_to_all(hidden, 'seq', split_axis=1, concat_axis=0, tiled=True)  19.4 us
  transfers between devices with their start and end apart: 5, of which 5 were waited for; matrix products, arithmetic and copies ran while one was open for 5% of the time, Pallas kernels for 0%

profile of v1, /device:TPU:1, one launch (start us, length us, event | category | flops | bytes accessed | tf_op | source)
XLA Modules:
  0.0 638.4 jit_solution(1461534168892707439)
XLA Ops:
  7.2 0.0 copy-start
  7.2 3.1 copy.85
  10.3 0.0 copy-start.6
  10.3 39.3 %all_to_all.60 = bf16[8,1024,128]{2,0,1:T(8,128)(2,1)S(1)} all-to-all(bf16[8,1024,128]{2,0,1:T(8,128)(2,1)S(1)} %copy.85), channel_id=1, replica_groups=mesh['seq'=32,'ch'=4] {'seq'}, dimensions={1} | all-to-all | bytes 4194304 | tf_op jit(solution)/shard_map/all_to_all | solution.py:32
  49.6 0.0 copy-start.2
  49.6 1.4 copy-done.2
  51.0 0.0 copy-done.6
  51.0 0.7 fusion.14
  51.7 2.7 copy.89
  54.4 4.8 all-to-all-start.3
  59.2 4.1 copy.78
  63.3 23.5 %all-to-all-done.3 = bf16[256,32,128]{2,1,0:T(8,128)(2,1)} async-done(((bf16[256,32,128]{2,1,0:T(8,128)(2,1)}), bf16[256,32,128]{2,1,0:T(8,128)(2,1)}, u32[]{:S(2)}, u32[]{:S(2)}) %all-to-all-start.3) | async-done | bytes 2097184 | tf_op jit(solution)/shard_map/all_to_all | solution.py:36
  86.8 2.1 convert_bitcast_fusion
  88.9 2.6 copy.90
  91.6 5.4 copy.91
  97.0 0.0 copy-done
  97.0 8.7 %fusion.2 = (bf16[8,1024,128]{1,2,0:T(8,128)(2,1)}, bf16[8,1024,128]{1,2,0:T(8,128)(2,1)}, bf16[8,1024,128]{1,2,0:T(8,128)(2,1)}) fusion(f32[8,1024,128]{1,2,0:T(8,128)} %copy.91, f32[8,1024,128]{1,2,0:T(8,128)} %copy.78, bf16[8,1024,128]{2,1,0:T(8,128)(2,1)S(1)} %bitcast.69, bf16[1024,1024]{1,0:T(8,128)(2,1)} %param.8), kind=kOutput, calls=%fused_computation.5 | convolution fusion | flops 2163212288 | bytes 18874368 | tf_op jit(solution)/shard_map/jk,ikc->ijc/dot_general | solution.py:22
  105.7 4.2 copy.79
  109.8 4.8 all-to-all-start
  114.6 0.2 all-reduce.5.cloned.1.call-start
  114.8 6.0 convolution_bitcast_fusion
  120.8 19.4 %all-to-all-done = bf16[8,1024,128]{2,0,1:T(8,128)(2,1)} async-done(((bf16[8,1024,128]{2,0,1:T(8,128)(2,1)}), bf16[8,1024,128]{2,0,1:T(8,128)(2,1)}, u32[]{:S(2)}, u32[]{:S(2)}) %all-to-all-start) | async-done | bytes 2097184 | tf_op jit(solution)/shard_map/all_to_all | solution.py:27
  140.2 0.0 copy-start.3
  140.2 2.2 copy.81
  142.4 0.0 copy-start.4
  142.4 1.3 copy-done.4
  143.7 0.0 copy-done.3
  143.7 1.7 fusion.21
  145.4 0.0 all-reduce.5.cloned.1.call-update
  145.4 0.0 all-reduce.7.cloned.1.call-start
  145.5 345.5 %all-reduce.5.cloned.1.call-done = (f32[1024,1024]{1,0:T(8,128)}, f32[256,256]{0,1:T(8,128)}) async-done(((f32[1024,1024]{1,0:T(8,128)}, f32[256,256]{0,1:T(8,128)}), (f32[1024,1024]{1,0:T(8,128)}, f32[256,256]{0,1:T(8,128)})) %all-reduce.5.cloned.1.call-update) | async-done | bytes 4456464 | tf_op jit(solution)/shard_map/psum | solution.py:8
  490.9 0.0 copy-start.5
  490.9 0.0 all-reduce.7.cloned.1.call-update
  490.9 1.6 copy-done.5
  492.5 3.0 convert_bitcast_fusion.2
  495.5 4.5 copy.83
  500.0 7.5 %all-to-all-start.1 = ((bf16[256,32,128]{2,1,0:T(8,128)(2,1)}), bf16[256,32,128]{2,1,0:T(8,128)(2,1)S(1)}, u32[]{:S(2)}, u32[]{:S(2)}) async-start(bf16[256,32,128]{2,1,0:T(8,128)(2,1)} %copy.83), calls=%async_computation.1 | async-start | bytes 4194304 | tf_op jit(solution)/shard_map/all_to_all | solution.py:31
  507.5 3.9 copy.95
  511.4 5.9 convert_bitcast_fusion.1
  517.3 3.9 copy.92
  521.2 4.5 all-to-all-done.1
  525.7 1.8 copy.84
  527.5 97.9 %all-reduce.7.cloned.1.call-done = (f32[1024,1024]{1,0:T(8,128)}, f32[256,256]{0,1:T(8,128)}) async-done(((f32[1024,1024]{1,0:T(8,128)}, f32[256,256]{0,1:T(8,128)}), (f32[1024,1024]{1,0:T(8,128)}, f32[256,256]{0,1:T(8,128)})) %all-reduce.7.cloned.1.call-update) | async-done | bytes 4456464 | tf_op jit(solution)/shard_map/psum | solution.py:9
  625.4 0.0 copy-start.7
  625.4 5.3 broadcast_multiply_fusion
  630.7 0.0 copy-done.7
  630.7 0.8 copy.98
  631.6 0.0 copy-done.1
  (2 shorter events, 0.0 us)
Async XLA Ops:
  7.2 89.8 %copy-start = (bf16[8192,128]{1,0:T(8,128)(2,1)S(1)}, bf16[8192,128]{1,0:T(8,128)(2,1)}, u32[]{:S(2)}) copy-start(bf16[8192,128]{1,0:T(8,128)(2,1)} %param.5) | copy-start | bytes 6291460
  10.3 40.7 %copy-start.6 = (bf16[256,256]{1,0:T(8,128)(2,1)S(1)}, bf16[256,256]{1,0:T(8,128)(2,1)}, u32[]{:S(2)}) copy-start(bf16[256,256]{1,0:T(8,128)(2,1)} %param.9) | copy-start | bytes 393220
  49.6 1.4 copy-start.2
  54.4 32.4 %all-to-all-start.3 = ((bf16[256,32,128]{2,1,0:T(8,128)(2,1)}), bf16[256,32,128]{2,1,0:T(8,128)(2,1)}, u32[]{:S(2)}, u32[]{:S(2)}) async-start(bf16[256,32,128]{2,1,0:T(8,128)(2,1)} %copy.89), calls=%async_computation.3 | async-start | bytes 4194304 | tf_op jit(solution)/shard_map/all_to_all | solution.py:36
  109.8 30.4 %all-to-all-start = ((bf16[8,1024,128]{2,0,1:T(8,128)(2,1)}), bf16[8,1024,128]{2,0,1:T(8,128)(2,1)}, u32[]{:S(2)}, u32[]{:S(2)}) async-start(bf16[8,1024,128]{2,0,1:T(8,128)(2,1)} %copy.79), calls=%async_computation | async-start | bytes 4194304 | tf_op jit(solution)/shard_map/all_to_all | solution.py:27
  114.6 376.3 %all-reduce.5.cloned.1.call-start = ((), (), s32[]{:S(2)}) async-start(), calls=%async_computation.4 | async-start | bytes 8912896 | tf_op jit(solution)/shard_map/psum | solution.py:8
  140.2 3.5 copy-start.3
  142.4 1.3 copy-start.4
  145.4 480.0 %all-reduce.7.cloned.1.call-start = ((), (), s32[]{:S(2)}) async-start(), calls=%async_computation.5 | async-start | bytes 8912896 | tf_op jit(solution)/shard_map/psum | solution.py:9
  490.9 1.6 copy-start.5
  500.0 25.7 %all-to-all-start.1 = ((bf16[256,32,128]{2,1,0:T(8,128)(2,1)}), bf16[256,32,128]{2,1,0:T(8,128)(2,1)S(1)}, u32[]{:S(2)}, u32[]{:S(2)}) async-start(bf16[256,32,128]{2,1,0:T(8,128)(2,1)} %copy.83), calls=%async_computation.1 | async-start | bytes 4194304 | tf_op jit(solution)/shard_map/all_to_all | solution.py:31
  625.4 5.3 copy-start.7
  625.4 6.1 copy-start.1
Sparse Core Ops, SparseCore 0:
  145.5 345.3 all-reduce.4
  493.5 131.8 all-reduce.6
